TPU v7x, 32 devices: a whole 2x2x4 slice. The times are simulated.
32 devices in a mesh: seq: 8 (over z, x), var: 4 (over y, core).
Axes of the slice: x: 2, y: 2, z: 4, core: 2. Of those that a mesh axis runs over, the one named last changes fastest.
Arguments:
- clean_proj: bfloat16 [256, 10240], P('seq'), may hold values from -8 to 8
- corrupt_proj: bfloat16 [256, 10240], P('seq'), may hold values from -8 to 8
- patch_pos: int32 [4, 16], P('var'), may hold values from 0 to 255
- patch_mode: int32 [4], P('var'), may hold values from 0 to 2
- a_log: float32 [16, 5120], replicated, may hold values from -6 to 1.5
- dt_bias: float32 [5120], replicated, may hold values from -6 to -2
- conv_weight: float32 [4, 5120], replicated, may hold values from -3 to 3
- conv_bias: float32 [5120], replicated, may hold values from -3 to 3
- x_weight: bfloat16 [5120, 192], replicated, may hold values from -0.078125 to 0.078125
- dt_weight: bfloat16 [160, 5120], replicated, may hold values from -0.5 to 0.5
- d_skip: float32 [5120], replicated, may hold values from 0.5 to 1.5
Outputs:
- patched_out: bfloat16 [4, 256, 5120], P('var', 'seq')
- effect_peak: float32 [4, 5120], P('var')
Inputs may be any that keep to these rules, and one draw needn't show every extreme that they name: `patch_pos`: positions of one variant may repeat.
All inputs are finite; a program needn't handle non-finite values.
Results may differ from a plain program's by a relative error of at most 0.0029.
The roundings to bfloat16 on the way count: a program that leaves them out, or rounds other values in their place, can miss the bound.
Values may be sent and summed in bfloat16 or wider, within the bound.
A program may use at most 128 MiB of HBM per device.

v0:
```python
import jax
import jax.numpy as jnp
from jax import lax
from jax.sharding import PartitionSpec as P

STATE = 16
RANK = 160
BLOCK = 8


tiny_offset = 1e-06


def from_behind(value, axis, steps):
    count = lax.axis_size(axis)
    first, last = (max(0, -steps), min(count, count - steps))
    return lax.ppermute(value, axis, [(source, source + steps) for source in range(first, last)])


def prefix(value, axis, combine, identity):
    size, place = (lax.axis_size(axis), lax.axis_index(axis))
    everything = jax.tree.map(lambda part: lax.all_gather(part, axis), value)
    start = jax.tree.map(
        lambda part, zero: jnp.broadcast_to(jnp.asarray(zero, part.dtype), part.shape),
        value,
        identity,
    )

    def hop(k, before):
        reached = k < place
        new = combine(before, jax.tree.map(lambda part: part[k], everything))
        return jax.tree.map(lambda a, b: jnp.where(reached, a, b), new, before)

    return lax.fori_loop(0, size, hop, start)


def merged(part, axis, combine):
    gathered = jax.tree.map(lambda a: lax.all_gather(a, axis), part)

    def take(source):
        return jax.tree.map(lambda a: lax.dynamic_index_in_dim(a, source, 0, False), gathered)

    return lax.fori_loop(
        1, lax.axis_size(axis), lambda source, state: combine(state, take(source)), take(0)
    )


def prepare(signal_rows, rim_rows, conv_weight, conv_bias, x_weight):
    row_count = signal_rows.shape[0]
    kernel = conv_weight.shape[0]
    padded = jnp.concatenate([rim_rows, signal_rows], axis=0).astype(jnp.float32)
    conv_sum = conv_bias[None, :] + conv_weight[0][None, :] * padded[0:row_count]
    for lag_index in range(1, kernel):
        conv_sum = (
            conv_sum + conv_weight[lag_index][None, :] * padded[lag_index : lag_index + row_count]
        )
    conv_act = lax.optimization_barrier(jax.nn.silu(conv_sum).astype(jnp.bfloat16))
    projected = jnp.dot(conv_act, x_weight, preferred_element_type=jnp.float32)
    low_rank = projected[:, :RANK].astype(jnp.bfloat16)
    input_map = projected[:, RANK : RANK + STATE]
    output_map = projected[:, RANK + STATE :]
    return (conv_act, low_rank, input_map, output_map)


def channels(parts, gate_rows, offset, span, a_log, dt_bias, dt_weight, d_skip):
    conv_act, low_rank, input_map, output_map = parts
    signal_f = lax.dynamic_slice_in_dim(conv_act, offset, span, 1).astype(jnp.float32)
    weight_cut = lax.dynamic_slice_in_dim(dt_weight, offset, span, 1)
    bias_cut = lax.dynamic_slice_in_dim(dt_bias, offset, span, 0)
    step_size = jax.nn.softplus(
        jnp.dot(low_rank, weight_cut, preferred_element_type=jnp.float32) + bias_cut[None, :]
    )
    decay_rates = jnp.exp(lax.dynamic_slice_in_dim(a_log, offset, span, 1))
    gate_act = jax.nn.silu(lax.dynamic_slice_in_dim(gate_rows, offset, span, 1).astype(jnp.float32))
    skip_cut = lax.dynamic_slice_in_dim(d_skip, offset, span, 0)
    return (step_size, signal_f, input_map, output_map, decay_rates, gate_act, skip_cut)


def local_pass(terms):
    step_size, signal_f, input_map, output_map, decay_rates, gate_act, skip_cut = terms
    row_count, span = step_size.shape
    blocks = row_count // BLOCK
    inflow = step_size * signal_f
    pieces = (
        step_size.reshape(blocks, BLOCK, span),
        inflow.reshape(blocks, BLOCK, span),
        input_map.reshape(blocks, BLOCK, STATE),
        output_map.reshape(blocks, BLOCK, STATE),
    )

    def advance(state, block_rows):
        steps, flows, b_rows, c_rows = block_rows
        outputs = []
        for row in range(BLOCK):
            state = (
                jnp.exp(-steps[row][None, :] * decay_rates) * state
                + flows[row][None, :] * b_rows[row][:, None]
            )
            outputs.append(jnp.sum(c_rows[row][:, None] * state, axis=0))
        return (state, jnp.stack(outputs))

    end_state, readout = lax.scan(advance, jnp.zeros((STATE, span), jnp.float32), pieces)
    running = jnp.cumsum(step_size, axis=0)
    return (readout.reshape(row_count, span), running, end_state)


def make_chain(rate_list):

    def chain(earlier, later):
        joined = ()
        for member, rates in enumerate(rate_list):
            early_first, early_state = (earlier[2 * member], earlier[2 * member + 1])
            late_first, late_state = (later[2 * member], later[2 * member + 1])
            joined = joined + (early_first * late_first, late_first * early_state + late_state)
        return joined

    return chain


def finish(terms, local_readout, running, incoming):
    step_size, signal_f, input_map, output_map, decay_rates, gate_act, skip_cut = terms
    readout = local_readout
    for entry in range(STATE):
        entering = jnp.exp(-decay_rates[entry][None, :] * running)
        readout = readout + output_map[:, entry : entry + 1] * entering * incoming[entry][None, :]
    return ((readout + skip_cut[None, :] * signal_f) * gate_act).astype(jnp.bfloat16)


def combine_stats(first_pair, second_pair):
    return (jnp.maximum(first_pair[0], second_pair[0]), first_pair[1] + second_pair[1])


def shards(
    clean_proj,
    corrupt_proj,
    patch_pos,
    patch_mode,
    a_log,
    dt_bias,
    conv_weight,
    conv_bias,
    x_weight,
    dt_weight,
    d_skip,
):
    row_count = clean_proj.shape[0]
    inner_dim = conv_weight.shape[1]
    margin = conv_weight.shape[0] - 1
    first_row = lax.axis_index("seq") * row_count
    positions = first_row + jnp.arange(row_count, dtype=jnp.int32)
    rim_positions = first_row - margin + jnp.arange(margin, dtype=jnp.int32)
    targets = patch_pos[0]
    chosen_mode = patch_mode[0]
    hits_here = jnp.any(positions[:, None] == targets[None, :], axis=1)
    hits_rim = jnp.any(rim_positions[:, None] == targets[None, :], axis=1)
    take_signal = hits_here & (chosen_mode != 1)
    take_gate = hits_here & (chosen_mode != 0)
    rim_signal = hits_rim & (chosen_mode != 1)
    clean_signal = clean_proj[:, :inner_dim]
    corrupt_signal = corrupt_proj[:, :inner_dim]
    clean_gate = clean_proj[:, inner_dim:]
    corrupt_gate = corrupt_proj[:, inner_dim:]
    tails = jnp.stack([clean_signal[row_count - margin :], corrupt_signal[row_count - margin :]])
    rims = from_behind(tails, "seq", 1)
    patched_signal = jnp.where(take_signal[:, None], clean_signal, corrupt_signal)
    patched_gate = jnp.where(take_gate[:, None], clean_gate, corrupt_gate)
    patched_rim = jnp.where(rim_signal[:, None], rims[0], rims[1])
    clean_front = prepare(clean_signal, rims[0], conv_weight, conv_bias, x_weight)
    corrupt_front = prepare(corrupt_signal, rims[1], conv_weight, conv_bias, x_weight)
    patched_front = prepare(patched_signal, patched_rim, conv_weight, conv_bias, x_weight)
    span = inner_dim // lax.axis_size("var")
    offset = lax.axis_index("var") * span
    clean_terms = channels(clean_front, clean_gate, offset, span, a_log, dt_bias, dt_weight, d_skip)
    corrupt_terms = channels(
        corrupt_front, corrupt_gate, offset, span, a_log, dt_bias, dt_weight, d_skip
    )
    patched_terms = channels(
        patched_front, patched_gate, 0, inner_dim, a_log, dt_bias, dt_weight, d_skip
    )
    run_terms = (clean_terms, corrupt_terms, patched_terms)
    locals_list = []
    summaries = ()
    identity = ()
    for terms in run_terms:
        local_readout, running, end_state = local_pass(terms)
        locals_list.append((local_readout, running))
        last_total = running[running.shape[0] - 1]
        summaries = summaries + (jnp.exp(-terms[4] * last_total[None, :]), end_state)
        identity = identity + (jnp.ones_like(end_state), jnp.zeros_like(end_state))
    chain = make_chain([terms[4] for terms in run_terms])
    incoming = prefix(summaries, "seq", chain, identity)
    clean_cut = finish(clean_terms, locals_list[0][0], locals_list[0][1], incoming[1])
    corrupt_cut = finish(corrupt_terms, locals_list[1][0], locals_list[1][1], incoming[3])
    patched_rows = finish(patched_terms, locals_list[2][0], locals_list[2][1], incoming[5])
    corrupt_whole = lax.all_gather(corrupt_cut, "var", axis=1, tiled=True)
    clean_cut, corrupt_cut, corrupt_whole, patched_rows = lax.optimization_barrier(
        (clean_cut, corrupt_cut, corrupt_whole, patched_rows)
    )
    sum_squares = jnp.sum(
        (clean_cut.astype(jnp.float32) - corrupt_cut.astype(jnp.float32)) ** 2, axis=0
    )
    peak = jnp.max(
        jnp.abs(patched_rows.astype(jnp.float32) - corrupt_whole.astype(jnp.float32)), axis=0
    )
    peak_all, squares_all = merged((peak, sum_squares), "seq", combine_stats)
    squares_all = lax.all_gather(squares_all, "var", axis=0, tiled=True)
    spread = jnp.sqrt(squares_all / (row_count * lax.axis_size("seq")) + tiny_offset)
    return (patched_rows[None], (peak_all / spread)[None])


def solution(mesh):
    return jax.shard_map(
        shards,
        mesh=mesh,
        in_specs=(
            P("seq", None),
            P("seq", None),
            P("var", None),
            P("var"),
            P(),
            P(),
            P(),
            P(),
            P(),
            P(),
            P(),
        ),
        out_specs=(P("var", "seq", None), P("var", None)),
        check_vma=False,
    )
```

profile of v0, /device:TPU:0, one launch (start us, length us, event | category | flops | bytes accessed | tf_op | source)
XLA Modules:
  0.0 363.3 jit_solution(16203284275749533660)
XLA Ops:
  9.3 4.9 %collective-permute-start = (bf16[2,3,5120]{2,1,0:T(4,128)(2,1)S(1)}, bf16[2,3,5120]{2,1,0:T(4,128)(2,1)S(1)}, u32[]{:S(2)}, u32[]{:S(2)}) collective-permute-start(bf16[2,3,5120]{2,1,0:T(4,128)(2,1)S(1)} %pad_maximum_fusion), channel_id=1, source_target_pairs={{0,4},{4,8},{8,12},{12,16},{16,20},{20,24},{24,28},{1,5},{5,9},{9,... | collective-permute-start | bytes 184328 | tf_op jit(solution)/shard_map/ppermute | solution.py:17
  16.4 1.2 fusion.127
  18.1 2.3 fusion.124
  21.3 1.4 dynamic_slice.142
  25.1 1.3 multiply_convert_fusion
  31.8 1.5 compare_select_fusion
  33.3 1.7 reduce_window_sum.29
  35.0 1.4 slice_reduce_fusion.49
  36.4 1.7 fusion.58
  38.1 2.0 fusion.22
  40.1 2.5 reduce_window_sum.30
  43.5 1.6 multiply_exponential_fusion.1
  45.1 1.8 fusion.126
  47.0 33.7 %while.77 = (s32[]{:T(128)}, f32[16,5120]{1,0:T(8,128)S(1)}, f32[4,8,5120]{2,1,0:T(8,128)}, f32[4,8,5120]{2,1,0:T(8,128)}, f32[16,5120]{1,0:T(8,128)S(1)}, /*ind...) while((s32[]{:T(128)}, f32[16,5120]{1,0:T(8,128)S(1)}, ...), condition=%wide.region_34.35_spmd.clone, body=%wide.region_25.34_spmd.clone.sunk | while | flops 5734410 | bytes 5944940 | solution.py:102
  47.7 2.5 dynamic-slice_negate_fusion.25
  50.2 1.3 multiply_reduce_fusion.40
  53.5 1.1 stack.157
  56.0 2.6 dynamic-slice_negate_fusion.25
  58.7 1.3 multiply_reduce_fusion.40
  62.0 1.1 stack.157
  64.4 2.5 dynamic-slice_negate_fusion.25
  66.9 1.3 multiply_reduce_fusion.40
  70.2 1.1 stack.157
  72.7 2.9 dynamic-slice_negate_fusion.25
  75.6 1.3 multiply_reduce_fusion.40
  78.9 1.1 stack.157
  81.4 12.8 %while.75 = (s32[]{:T(128)}, f32[16,1280]{1,0:T(8,128)S(1)}, f32[4,8,1280]{2,1,0:T(8,128)S(1)}, f32[4,8,1280]{2,1,0:T(8,128)}, f32[16,1280]{1,0:T(8,128)S(1)}, /...) while((s32[]{:T(128)}, f32[16,1280]{1,0:T(8,128)S(1)}, ...), condition=%wide.region_9.10_spmd.clone, body=%wide.region_0.9_spmd.clone.sunk | while | flops 1433610 | bytes 1572460 | solution.py:102
  82.1 1.8 dynamic-slice_reduce_fusion.21
  85.3 1.8 dynamic-slice_reduce_fusion.21
  88.5 1.8 dynamic-slice_reduce_fusion.21
  91.7 1.7 dynamic-slice_reduce_fusion.21
  94.9 14.8 %while.76 = (s32[]{:T(128)}, f32[16,1280]{1,0:T(8,128)S(1)}, f32[4,8,1280]{2,1,0:T(8,128)}, f32[4,8,1280]{2,1,0:T(8,128)}, f32[16,1280]{1,0:T(8,128)S(1)}, /*ind...) while((s32[]{:T(128)}, f32[16,1280]{1,0:T(8,128)S(1)}, ...), condition=%wide.region_21.22_spmd.clone, body=%wide.region_12.21_spmd.clone.sunk | while | flops 1433610 | bytes 1572460 | solution.py:102
  95.6 1.8 dynamic-slice_reduce_fusion.22
  99.4 1.7 dynamic-slice_reduce_fusion.22
  103.2 1.8 dynamic-slice_reduce_fusion.22
  106.9 1.5 dynamic-slice_reduce_fusion.22
  114.0 35.9 %all-gather = f32[128,1280]{1,0:T(8,128)} all-gather(f32[16,1280]{1,0:T(8,128)S(1)} %multiply_exponential_fusion.2), channel_id=2, replica_groups=mesh['seq'=8,'var'=4] {'seq'}, dimensions={0}, use_global_device_ids=true | all-gather | bytes 737280 | tf_op jit(solution)/shard_map/all_gather | solution.py:22
  149.9 35.1 %all-gather.2 = f32[128,1280]{1,0:T(8,128)} all-gather(f32[16,1280]{1,0:T(8,128)S(1)} %copy-done.13), channel_id=4, replica_groups=mesh['seq'=8,'var'=4] {'seq'}, dimensions={0}, use_global_device_ids=true | all-gather | bytes 737280 | tf_op jit(solution)/shard_map/all_gather | solution.py:22
  185.1 33.7 %all-gather.3 = f32[128,1280]{1,0:T(8,128)} all-gather(f32[16,1280]{1,0:T(8,128)S(1)} %get-tuple-element.456), channel_id=5, replica_groups=mesh['seq'=8,'var'=4] {'seq'}, dimensions={0}, use_global_device_ids=true | all-gather | bytes 737280 | tf_op jit(solution)/shard_map/all_gather | solution.py:22
  218.8 33.4 %all-gather.1 = f32[128,1280]{1,0:T(8,128)} all-gather(f32[16,1280]{1,0:T(8,128)S(1)} %get-tuple-element.455), channel_id=3, replica_groups=mesh['seq'=8,'var'=4] {'seq'}, dimensions={0}, use_global_device_ids=true | all-gather | bytes 737280 | tf_op jit(solution)/shard_map/all_gather | solution.py:22
  253.2 19.9 %while.78 = (s32[]{:T(128)}, f32[16,1280]{1,0:T(8,128)S(1)}, f32[16,1280]{1,0:T(8,128)S(1)}, f32[16,5120]{1,0:T(8,128)S(1)}, s32[]{:T(128)}, /*index=5*/f32[8,16...) while((s32[]{:T(128)}, f32[16,1280]{1,0:T(8,128)S(1)}, ...), condition=%wide.region_36.37_spmd.clone, body=%wide.region_35.36_spmd.clone.sunk | while | flops 491524 | bytes 1966243 | solution.py:34
  253.2 1.2 fusion.140
  254.4 1.4 fusion.141
  255.8 1.1 fusion.140
  256.9 1.4 fusion.141
  258.3 1.1 fusion.140
  259.4 1.4 fusion.141
  260.7 1.1 fusion.140
  261.8 1.4 fusion.141
  263.2 1.1 fusion.140
  264.3 1.4 fusion.141
  265.7 1.1 fusion.140
  266.8 1.4 fusion.141
  268.1 1.1 fusion.140
  269.2 1.4 fusion.141
  270.6 1.1 fusion.140
  271.7 1.4 fusion.141
  274.2 1.8 fusion.65
  276.0 6.4 %all_gather.66 = bf16[32,5120]{1,0:T(8,128)(2,1)S(1)} all-gather(bf16[32,1280]{1,0:T(8,128)(2,1)S(1)} %fusion.65), channel_id=1, replica_groups=mesh['seq'=8,'var'=4] {'var'}, dimensions={1}, use_global_device_ids=true | all-gather | bytes 409600 | tf_op jit(solution)/shard_map/all_gather | solution.py:195
  282.5 1.8 fusion.61
  284.4 3.8 %fusion.25 = bf16[32,5120]{1,0:T(8,128)(2,1)S(1)} fusion(bf16[32,5120]{1,0:T(8,128)(2,1)S(1)} %copy-done.3, f32[4,8,5120]{2,1,0:T(8,128)} %get-tuple-element.461, f32[32,5120]{1,0:T(8,128)S(1)} %copy-done.11, f32[5120]{0:T(1024)S(1)} %copy-done.51, f32[5120]{0:T(1024)S(1)} %bitcast.504, f32[5120]{0:T(1024)S(1)} %bitcast.489, f32[32]{0:T(128)S(1)} %copy-done.53, ...), kind=kLoop, calls=%fused_computation.194 | loop fusion | flops 12288000 | bytes 3299360 | tf_op jit(solution)/shard_map/convert_element_type | solution.py:126
  288.3 30.7 %all-gather.8 = f32[8,1,1280]{2,1,0:T(1,128)S(1)} all-gather(f32[1,1,1280]{2,1,0:T(1,128)S(1)} %reshape.510), channel_id=9, replica_groups=mesh['seq'=8,'var'=4] {'seq'}, dimensions={0}, use_global_device_ids=true | all-gather | bytes 46080 | tf_op jit(solution)/shard_map/all_gather | solution.py:38
  319.2 30.6 %all-gather.6 = f32[40960]{0:T(1024)S(1)} all-gather(f32[5120]{0:T(1024)S(1)} %abs_reduce_fusion), channel_id=8, replica_groups=mesh['seq'=8,'var'=4] {'seq'}, dimensions={0}, use_global_device_ids=true | all-gather | bytes 184320 | tf_op jit(solution)/shard_map/all_gather | solution.py:38
  350.6 5.2 %all-gather.9 = f32[4,1,1280]{2,1,0:T(1,128)S(1)} all-gather(f32[1,1,1280]{2,1,0:T(1,128)S(1)} %reshape.512), channel_id=1, replica_groups=mesh['seq'=8,'var'=4] {'var'}, dimensions={0}, use_global_device_ids=true | all-gather | bytes 25600 | tf_op jit(solution)/shard_map/all_gather | solution.py:206
  (364 shorter events, 49.9 us)
Async XLA Ops:
  7.2 19.2 %copy-start = (bf16[5120,192]{0,1:T(8,128)(2,1)S(1)}, bf16[5120,192]{0,1:T(8,128)(2,1)}, u32[]{:S(2)}) copy-start(bf16[5120,192]{0,1:T(8,128)(2,1)} %param.29) | copy-start | bytes 5898244
  7.2 245.9 %all-gather.13.cloned.1.call-start = ((), (), s32[]{:S(2)}) async-start(), calls=%async_computation | async-start | bytes 2949120 | tf_op jit(solution)/shard_map/all_gather | solution.py:22
  9.3 13.4 %collective-permute-start = (bf16[2,3,5120]{2,1,0:T(4,128)(2,1)S(1)}, bf16[2,3,5120]{2,1,0:T(4,128)(2,1)S(1)}, u32[]{:S(2)}, u32[]{:S(2)}) collective-permute-start(bf16[2,3,5120]{2,1,0:T(4,128)(2,1)S(1)} %pad_maximum_fusion), channel_id=1, source_target_pairs={{0,4},{4,8},{8,12},{12,16},{16,20},{20,24},{24,28},{1,5},{5,9},{9,... | collective-permute-start | bytes 184328 | tf_op jit(solution)/shard_map/ppermute | solution.py:17
  20.4 4.6 %copy-start.19 = (f32[5120]{0:T(1024)S(1)}, f32[5120]{0:T(1024)}, u32[]{:S(2)}) copy-start(f32[5120]{0:T(1024)} %param.28) | copy-start | bytes 61444
  26.3 1.5 copy-start.7
  26.3 1.5 copy-start.8
  26.3 11.8 %copy-start.2 = (bf16[32,5120]{1,0:T(8,128)(2,1)}, bf16[32,5120]{1,0:T(8,128)(2,1)S(1)}, u32[]{:S(2)}) copy-start(bf16[32,5120]{1,0:T(8,128)(2,1)S(1)} %get-tuple-element.964) | copy-start | bytes 983044
  26.4 2.8 copy-start.54
  27.8 4.0 %copy-start.50 = (f32[5120]{0:T(1024)S(1)}, f32[5120]{0:T(1024)}, u32[]{:S(2)}) copy-start(f32[5120]{0:T(1024)} %param.26) | copy-start | bytes 61444
  30.4 6.0 %copy-start.5 = (f32[32,1280]{1,0:T(8,128)}, f32[32,1280]{1,0:T(8,128)S(1)}, u32[]{:S(2)}) copy-start(f32[32,1280]{1,0:T(8,128)S(1)} %compare_select_fusion.2) | copy-start | bytes 491524
  38.1 5.4 %copy-start.18 = (f32[1280]{0:T(1024)S(1)}, f32[1280]{0:T(1024)}, u32[]{:S(2)}) copy-start(f32[1280]{0:T(1024)} %slice_reduce_fusion.49) | copy-start | bytes 15364
  46.9 206.2 %all-gather.15.cloned.1.call-start = ((), (), s32[]{:S(2)}) async-start(), calls=%async_computation.1 | async-start | bytes 2949120 | tf_op jit(solution)/shard_map/all_gather | solution.py:22
  80.7 0.7 copy-start.1
  94.2 0.7 copy-start.15
  94.9 14.8 %copy-start.6 = (f32[4,8,1280]{2,1,0:T(8,128)S(1)}, f32[4,8,1280]{2,1,0:T(8,128)}, u32[]{:S(2)}) copy-start(f32[4,8,1280]{2,1,0:T(8,128)} %get-tuple-element.1725) | copy-start | bytes 491524
  109.7 40.2 %copy-start.13 = (f32[16,1280]{1,0:T(8,128)S(1)}, f32[16,1280]{1,0:T(8,128)}, u32[]{:S(2)}) copy-start(f32[16,1280]{1,0:T(8,128)} %get-tuple-element.827) | copy-start | bytes 245764
  113.1 140.0 %copy-start.4 = (f32[16,1280]{1,0:T(8,128)S(1)}, f32[16,1280]{1,0:T(8,128)}, u32[]{:S(2)}) copy-start(f32[16,1280]{1,0:T(8,128)} %custom-call.3) | copy-start | bytes 245764
  253.1 21.0 %copy-start.14 = (f32[32,1280]{1,0:T(8,128)S(1)}, f32[32,1280]{1,0:T(8,128)}, u32[]{:S(2)}) copy-start(f32[32,1280]{1,0:T(8,128)} %reduce_window_sum.29) | copy-start | bytes 491524
  253.1 21.0 %copy-start.17 = (f32[4,8,1280]{2,1,0:T(8,128)S(1)}, f32[4,8,1280]{2,1,0:T(8,128)}, u32[]{:S(2)}) copy-start(f32[4,8,1280]{2,1,0:T(8,128)} %get-tuple-element.459) | copy-start | bytes 491524
  253.2 21.0 %copy-start.32 = (f32[1280]{0:T(1024)S(1)}, f32[1280]{0:T(1024)}, u32[]{:S(2)}) copy-start(f32[1280]{0:T(1024)} %dynamic_slice.142) | copy-start | bytes 15364
  253.2 21.0 %copy-start.33 = (f32[1280]{0:T(1024)S(1)}, f32[1280]{0:T(1024)}, u32[]{:S(2)}) copy-start(f32[1280]{0:T(1024)} %get-tuple-element.656) | copy-start | bytes 15364
  253.2 21.0 %copy-start.35 = (f32[1280]{0:T(1024)S(1)}, f32[1280]{0:T(1024)}, u32[]{:S(2)}) copy-start(f32[1280]{0:T(1024)} %get-tuple-element.657) | copy-start | bytes 15364
  273.1 9.3 %copy-start.16 = (f32[4,8,1280]{2,1,0:T(8,128)S(1)}, f32[4,8,1280]{2,1,0:T(8,128)}, u32[]{:S(2)}) copy-start(f32[4,8,1280]{2,1,0:T(8,128)} %copy-done.15) | copy-start | bytes 491524
  273.1 9.3 %copy-start.34 = (f32[1280]{0:T(1024)S(1)}, f32[1280]{0:T(1024)}, u32[]{:S(2)}) copy-start(f32[1280]{0:T(1024)} %get-tuple-element.656) | copy-start | bytes 15364
  273.1 9.3 %copy-start.36 = (f32[1280]{0:T(1024)S(1)}, f32[1280]{0:T(1024)}, u32[]{:S(2)}) copy-start(f32[1280]{0:T(1024)} %get-tuple-element.657) | copy-start | bytes 15364
  273.1 9.3 %copy-start.37 = (f32[1280]{0:T(1024)S(1)}, f32[1280]{0:T(1024)}, u32[]{:S(2)}) copy-start(f32[1280]{0:T(1024)} %get-tuple-element.658) | copy-start | bytes 15364
  273.1 9.3 %copy-start.38 = (f32[1280]{0:T(1024)S(1)}, f32[1280]{0:T(1024)}, u32[]{:S(2)}) copy-start(f32[1280]{0:T(1024)} %get-tuple-element.659) | copy-start | bytes 15364
  273.1 9.3 %copy-start.39 = (f32[1280]{0:T(1024)S(1)}, f32[1280]{0:T(1024)}, u32[]{:S(2)}) copy-start(f32[1280]{0:T(1024)} %get-tuple-element.660) | copy-start | bytes 15364
  273.1 9.3 %copy-start.40 = (f32[1280]{0:T(1024)S(1)}, f32[1280]{0:T(1024)}, u32[]{:S(2)}) copy-start(f32[1280]{0:T(1024)} %get-tuple-element.661) | copy-start | bytes 15364
  273.1 9.3 %copy-start.41 = (f32[1280]{0:T(1024)S(1)}, f32[1280]{0:T(1024)}, u32[]{:S(2)}) copy-start(f32[1280]{0:T(1024)} %get-tuple-element.662) | copy-start | bytes 15364
  273.2 9.3 %copy-start.42 = (f32[1280]{0:T(1024)S(1)}, f32[1280]{0:T(1024)}, u32[]{:S(2)}) copy-start(f32[1280]{0:T(1024)} %get-tuple-element.663) | copy-start | bytes 15364
  273.2 9.3 %copy-start.43 = (f32[1280]{0:T(1024)S(1)}, f32[1280]{0:T(1024)}, u32[]{:S(2)}) copy-start(f32[1280]{0:T(1024)} %get-tuple-element.664) | copy-start | bytes 15364
  273.2 9.3 %copy-start.44 = (f32[1280]{0:T(1024)S(1)}, f32[1280]{0:T(1024)}, u32[]{:S(2)}) copy-start(f32[1280]{0:T(1024)} %get-tuple-element.665) | copy-start | bytes 15364
  273.2 9.3 %copy-start.45 = (f32[1280]{0:T(1024)S(1)}, f32[1280]{0:T(1024)}, u32[]{:S(2)}) copy-start(f32[1280]{0:T(1024)} %get-tuple-element.666) | copy-start | bytes 15364
  273.2 9.3 %copy-start.46 = (f32[1280]{0:T(1024)S(1)}, f32[1280]{0:T(1024)}, u32[]{:S(2)}) copy-start(f32[1280]{0:T(1024)} %get-tuple-element.667) | copy-start | bytes 15364
  273.2 9.3 %copy-start.47 = (f32[1280]{0:T(1024)S(1)}, f32[1280]{0:T(1024)}, u32[]{:S(2)}) copy-start(f32[1280]{0:T(1024)} %get-tuple-element.668) | copy-start | bytes 15364
  273.2 9.3 %copy-start.48 = (f32[1280]{0:T(1024)S(1)}, f32[1280]{0:T(1024)}, u32[]{:S(2)}) copy-start(f32[1280]{0:T(1024)} %get-tuple-element.669) | copy-start | bytes 15364
  273.2 9.3 %copy-start.49 = (f32[1280]{0:T(1024)S(1)}, f32[1280]{0:T(1024)}, u32[]{:S(2)}) copy-start(f32[1280]{0:T(1024)} %get-tuple-element.670) | copy-start | bytes 15364
  273.5 10.8 %copy-start.3 = (bf16[32,5120]{1,0:T(8,128)(2,1)S(1)}, bf16[32,5120]{1,0:T(8,128)(2,1)}, u32[]{:S(2)}) copy-start(bf16[32,5120]{1,0:T(8,128)(2,1)} %copy-done.2) | copy-start | bytes 983044
  273.5 10.8 %copy-start.9 = (bf16[32,10240]{1,0:T(8,128)(2,1)S(1)}, bf16[32,10240]{1,0:T(8,128)(2,1)}, u32[]{:S(2)}) copy-start(bf16[32,10240]{1,0:T(8,128)(2,1)} %param.22) | copy-start | bytes 1966084
  273.5 10.8 %copy-start.10 = (bf16[32,10240]{1,0:T(8,128)(2,1)S(1)}, bf16[32,10240]{1,0:T(8,128)(2,1)}, u32[]{:S(2)}) copy-start(bf16[32,10240]{1,0:T(8,128)(2,1)} %param.21) | copy-start | bytes 1966084
  273.5 10.8 %copy-start.11 = (f32[32,5120]{1,0:T(8,128)S(1)}, f32[32,5120]{1,0:T(8,128)}, u32[]{:S(2)}) copy-start(f32[32,5120]{1,0:T(8,128)} %reduce_window_sum.30) | copy-start | bytes 1966084
  273.5 10.8 %copy-start.20 = (f32[1,5120]{1,0:T(1,128)S(1)}, f32[1,5120]{1,0:T(1,128)}, u32[]{:S(2)}) copy-start(f32[1,5120]{1,0:T(1,128)} %get-tuple-element.934) | copy-start | bytes 61444
  273.5 10.8 %copy-start.21 = (f32[1,5120]{1,0:T(1,128)S(1)}, f32[1,5120]{1,0:T(1,128)}, u32[]{:S(2)}) copy-start(f32[1,5120]{1,0:T(1,128)} %get-tuple-element.935) | copy-start | bytes 61444
  273.5 10.8 %copy-start.22 = (f32[1,5120]{1,0:T(1,128)S(1)}, f32[1,5120]{1,0:T(1,128)}, u32[]{:S(2)}) copy-start(f32[1,5120]{1,0:T(1,128)} %get-tuple-element.936) | copy-start | bytes 61444
  273.5 10.8 %copy-start.23 = (f32[1,5120]{1,0:T(1,128)S(1)}, f32[1,5120]{1,0:T(1,128)}, u32[]{:S(2)}) copy-start(f32[1,5120]{1,0:T(1,128)} %get-tuple-element.937) | copy-start | bytes 61444
  273.6 10.8 %copy-start.24 = (f32[1,5120]{1,0:T(1,128)S(1)}, f32[1,5120]{1,0:T(1,128)}, u32[]{:S(2)}) copy-start(f32[1,5120]{1,0:T(1,128)} %get-tuple-element.938) | copy-start | bytes 61444
  273.6 10.8 %copy-start.25 = (f32[1,5120]{1,0:T(1,128)S(1)}, f32[1,5120]{1,0:T(1,128)}, u32[]{:S(2)}) copy-start(f32[1,5120]{1,0:T(1,128)} %get-tuple-element.939) | copy-start | bytes 61444
  273.6 10.8 %copy-start.26 = (f32[1,5120]{1,0:T(1,128)S(1)}, f32[1,5120]{1,0:T(1,128)}, u32[]{:S(2)}) copy-start(f32[1,5120]{1,0:T(1,128)} %get-tuple-element.940) | copy-start | bytes 61444
  273.6 10.8 %copy-start.27 = (f32[1,5120]{1,0:T(1,128)S(1)}, f32[1,5120]{1,0:T(1,128)}, u32[]{:S(2)}) copy-start(f32[1,5120]{1,0:T(1,128)} %get-tuple-element.941) | copy-start | bytes 61444
  273.6 10.8 %copy-start.28 = (f32[1,5120]{1,0:T(1,128)S(1)}, f32[1,5120]{1,0:T(1,128)}, u32[]{:S(2)}) copy-start(f32[1,5120]{1,0:T(1,128)} %get-tuple-element.942) | copy-start | bytes 61444
  273.6 10.8 %copy-start.29 = (f32[1,5120]{1,0:T(1,128)S(1)}, f32[1,5120]{1,0:T(1,128)}, u32[]{:S(2)}) copy-start(f32[1,5120]{1,0:T(1,128)} %get-tuple-element.943) | copy-start | bytes 61444
  273.6 10.8 %copy-start.30 = (f32[1,5120]{1,0:T(1,128)S(1)}, f32[1,5120]{1,0:T(1,128)}, u32[]{:S(2)}) copy-start(f32[1,5120]{1,0:T(1,128)} %get-tuple-element.944) | copy-start | bytes 61444
  273.6 10.8 %copy-start.31 = (f32[1,5120]{1,0:T(1,128)S(1)}, f32[1,5120]{1,0:T(1,128)}, u32[]{:S(2)}) copy-start(f32[1,5120]{1,0:T(1,128)} %get-tuple-element.945) | copy-start | bytes 61444
  273.6 10.8 %copy-start.51 = (f32[5120]{0:T(1024)S(1)}, f32[5120]{0:T(1024)}, u32[]{:S(2)}) copy-start(f32[5120]{0:T(1024)} %param.31) | copy-start | bytes 61444
  273.6 10.8 %copy-start.52 = (f32[32]{0:T(128)S(1)}, f32[32]{0:T(128)}, u32[]{:S(2)}) copy-start(f32[32]{0:T(128)} %get-tuple-element.687) | copy-start | bytes 388
  273.7 10.8 %copy-start.53 = (f32[32]{0:T(128)S(1)}, f32[32]{0:T(128)}, u32[]{:S(2)}) copy-start(f32[32]{0:T(128)} %get-tuple-element.688) | copy-start | bytes 388
  288.2 68.2 %copy-start.12 = (bf16[32,5120]{1,0:T(8,128)(2,1)}, bf16[32,5120]{1,0:T(8,128)(2,1)S(1)}, u32[]{:S(2)}) copy-start(bf16[32,5120]{1,0:T(8,128)(2,1)S(1)} %fusion.25) | copy-start | bytes 983044
Sparse Core Ops, SparseCore 0:
  47.0 54.7 all-gather.12
  104.0 64.4 all-gather.14
where the time goes:
time: 366 us; the launch traced here: 363 us
  blocking collectives  211 us (58%)
  other arithmetic  90.6 us (25%)
  local copies, waits for them, and re-layouts  34.8 us (10%)
  between operations  15.7 us (4%)
  starting transfers between devices  4.95 us (1%)
  matrix products  4.74 us (1%)
    all_gather x4, blocking collectives, prefix(): everything = jax.tree.map(lambda part: lax.all_gather(part, axis), value)  138 us
    all_gather x2, blocking collectives, merged(): gathered = jax.tree.map(lambda a: lax.all_gather(a, axis), part)  61.3 us
    select_n x16, other arithmetic, hop(): return jax.tree.map(lambda a, b: jnp.where(reached, a, b), new, before)  19.7 us
    reduce_sum x36, other arithmetic, advance(): outputs.append(jnp.sum(c_rows[row][:, None] * state, axis=0))  17 us
    slice x8, other arithmetic, advance(): flows[row][None, :] * b_rows[row][:, None]  13.8 us
    neg x4, other arithmetic, advance(): -steps[row][None, :] * decay_rates  10.5 us
    dynamic_slice x12, local copies, waits for them, and re-layouts, local_pass(): lax.scan(advance, jnp.zeros((STATE, span), jnp.float32), pieces)  8.26 us
    convert_element_type x3, other arithmetic, finish(): ((readout + skip_cut[None, :] * signal_f) * gate_act).astype(jnp.bfloat16)  7.37 us
  transfers between devices with their start and end apart: 3, of which 0 were waited for; matrix products, arithmetic and copies ran while one was open for 20% of the time, Pallas kernels for 0%

commit v1 on v0

v1 whole, which is shorter than its diff:
```python
import functools

import jax
import jax.numpy as jnp
from jax import lax
from jax.experimental import pallas as pl
from jax.experimental.pallas import tpu as pltpu
from jax.sharding import PartitionSpec as P

STATE = 16
RANK = 160
PAD = 8
LOG2E = 1.4426950408889634
TINY = 1e-06
MESH = pl.DeviceIdType.MESH


def lanes(width, most):
    best = 128
    for k in range(1, most // 128 + 1):
        if width % (128 * k) == 0:
            best = 128 * k
    return best


def wide(tile, width):
    return jnp.concatenate([tile] * (width // 128), axis=1)


def body(
    ns, nv,
    clean, corrupt, pos, mode, a_log, dtb, cw, cb, xw, dtw, dsk,
    out, eff,
    tails, rims, ext, act16, act, proj, bsp, csp, rate, stp, acc, run, tot, tot_in,
    ends, even_end, carry, carry_out, cut, whole, own_sq, sq_in, own_pk, pk_in, nrm, nrm_in,
    s_rim, r_rim, s_tot, r_tot, s_even, r_even, s_car, r_car, s_cor, r_cor,
    s_sq, r_sq, s_pk, r_pk, s_nrm, r_nrm,
):
    rows = clean.shape[0]
    inner = cw.shape[1]
    taps = cw.shape[0]
    span = inner // nv
    s = lax.axis_index("seq")
    v = lax.axis_index("var")
    even = lax.rem(s, 2) == 0
    odd = lax.rem(s, 2) == 1

    barrier = pltpu.get_barrier_semaphore()

    def greet(d, _):
        pl.semaphore_signal(barrier, inc=1, device_id={"seq": lax.rem(s + d, ns)}, device_id_type=MESH)
        return 0

    lax.fori_loop(1, ns, greet, 0)
    for d in range(1, nv):
        pl.semaphore_signal(barrier, inc=1, device_id={"var": lax.rem(v + d, nv)}, device_id_type=MESH)

    tails[...] = jnp.concatenate(
        [
            clean[rows - 16 :, :inner].astype(jnp.float32)[8:],
            corrupt[rows - 16 :, :inner].astype(jnp.float32)[8:],
        ],
        axis=0,
    ).astype(jnp.bfloat16)
    pl.semaphore_wait(barrier, ns - 1 + nv - 1)

    def remote(src, dst, send, recv, where):
        return pltpu.make_async_remote_copy(
            src_ref=src, dst_ref=dst, send_sem=send, recv_sem=recv,
            device_id=where, device_id_type=MESH,
        )

    rim_copy = remote(tails, rims, s_rim, r_rim, {"seq": lax.rem(s + 1, ns)})

    @pl.when(s < ns - 1)
    def _():
        rim_copy.start()

    rate[...] = jnp.exp(a_log[...]) * (-LOG2E)
    where_rows = s * rows - PAD + lax.broadcasted_iota(jnp.int32, (rows + PAD, pos.shape[1]), 0)
    hits = jnp.max((where_rows == pos[...]).astype(jnp.float32), axis=1, keepdims=True)
    chosen = mode[...]
    take_signal = hits * (chosen != 1).astype(jnp.float32) > 0.5
    take_gate = (hits * (chosen != 0).astype(jnp.float32) > 0.5)[PAD:]

    @pl.when(s == 0)
    def _():
        rims[...] = jnp.zeros_like(rims)

    @pl.when(s > 0)
    def _():
        rim_copy.wait_recv()

    lb = lanes(inner, 256)

    def conv(i, _):
        col = pl.ds(pl.multiple_of(i * lb, lb), lb)
        edge = rims[:, col].astype(jnp.float32)
        ext[0, 0:PAD, :] = edge[0:8]
        ext[1, 0:PAD, :] = edge[8:16]
        ext[0, PAD:, :] = clean[:, col].astype(jnp.float32)
        ext[1, PAD:, :] = corrupt[:, col].astype(jnp.float32)
        ext[2] = jnp.where(take_signal, ext[0], ext[1])
        for r in range(3):
            total = cb[:, col] + cw[0:1, col] * ext[r, PAD - taps + 1 : PAD - taps + 1 + rows, :]
            for k in range(1, taps):
                first = PAD - taps + 1 + k
                total = total + cw[k : k + 1, col] * ext[r, first : first + rows, :]
            rounded = (total / (1.0 + jnp.exp(-total))).astype(jnp.bfloat16)
            act16[r * rows : (r + 1) * rows, col] = rounded
            act[r, :, col] = rounded.astype(jnp.float32)
        return 0

    lax.fori_loop(0, inner // lb, conv, 0)
    width = xw.shape[1]
    proj[...] = jnp.zeros_like(proj)
    proj[:, :width] = jnp.dot(act16[...], xw[...], preferred_element_type=jnp.float32)
    flipped = proj[:, 128:].T
    first = RANK - 128
    for t in range(3 * rows):
        bsp[t] = jnp.broadcast_to(flipped[first : first + STATE, t : t + 1], (STATE, 128))
        csp[t] = jnp.broadcast_to(flipped[first + STATE : first + 2 * STATE, t : t + 1], (STATE, 128))

    chunks = [(0, v * span), (1, v * span)] + [(2, j * span) for j in range(nv)]
    tb = lanes(span, 256)

    for c, (r, off) in enumerate(chunks):
        low = proj[r * rows : (r + 1) * rows, :RANK].astype(jnp.bfloat16)

        def steps_of(i, _, c=c, off=off, low=low):
            here = pl.ds(pl.multiple_of(i * tb, tb), tb)
            col = pl.ds(pl.multiple_of(off + i * tb, tb), tb)
            raw = jnp.dot(low, dtw[:, col], preferred_element_type=jnp.float32) + dtb[:, col]
            step = jnp.maximum(raw, 0.0) + jnp.log1p(jnp.exp(-jnp.abs(raw)))
            stp[c, :, here] = step
            tot[c, :, here] = jnp.sum(step, axis=0, keepdims=True)
            return 0

        lax.fori_loop(0, span // tb, steps_of, 0)

    partner = {"seq": lax.rem(s + 1, ns)}
    tot_copy = remote(tot, tot_in, s_tot, r_tot, partner)

    @pl.when(even)
    def _():
        tot_copy.start()

    even_copies = [remote(ends.at[c], even_end.at[c], s_even.at[c], r_even.at[c], partner) for c in range(len(chunks))]

    for c, (r, off) in enumerate(chunks):

        def scan_of(i, _, c=c, r=r, off=off):
            here = pl.ds(pl.multiple_of(i * tb, tb), tb)
            col = pl.ds(pl.multiple_of(off + i * tb, tb), tb)
            rates = rate[:, col]

            def eight(b, carried):
                state, running = carried
                at = pl.ds(pl.multiple_of(b * 8, 8), 8)
                steps = stp[c, at, here]
                flows = steps * act[r, at, col]
                outs, sums = [], []
                for k in range(8):
                    step = steps[k : k + 1]
                    t = r * rows + b * 8 + k
                    state = jnp.exp2(rates * step) * state + flows[k : k + 1] * wide(bsp[t], tb)
                    running = running + step
                    outs.append(jnp.sum(wide(csp[t], tb) * state, axis=0, keepdims=True))
                    sums.append(running)
                acc[c, at, here] = jnp.concatenate(outs, axis=0)
                run[c, at, here] = jnp.concatenate(sums, axis=0)
                return state, running

            zero = (jnp.zeros((STATE, tb), jnp.float32), jnp.zeros((1, tb), jnp.float32))
            state, _ = lax.fori_loop(0, rows // 8, eight, zero)
            ends[c, :, here] = state
            return 0

        lax.fori_loop(0, span // tb, scan_of, 0)

        @pl.when(even)
        def _(c=c):
            even_copies[c].start()

    @pl.when(odd)
    def _():
        tot_copy.wait_recv()

    onward = []
    for c in range(len(chunks)):
        onward.append(
            [
                remote(carry_out.at[c], carry.at[c], s_car.at[c, m], r_car.at[c], {"seq": lax.rem(s + 1 + m, ns)})
                for m in range(2)
            ]
        )

    cor_copies = [
        remote(cut.at[1], whole.at[d - 1], s_cor.at[d - 1], r_cor.at[d - 1], {"var": lax.rem(v + d, nv)})
        for d in range(1, nv)
    ]

    def seq_copy(d, src, dst, send, recv):
        return remote(src, dst.at[d - 1], send.at[d - 1], recv.at[d - 1], {"seq": lax.rem(s + d, ns)})

    def start_all(src, dst, send, recv):
        def go(d, _):
            seq_copy(d, src, dst, send, recv).start()
            return 0

        lax.fori_loop(1, ns, go, 0)

    def wait_all(src, dst, send, recv):
        def go(d, _):
            seq_copy(d, src, dst, send, recv).wait()
            return 0

        lax.fori_loop(1, ns, go, 0)

    for c, (r, off) in enumerate(chunks):

        @pl.when(s < 2)
        def _(c=c):
            carry[c] = jnp.zeros((STATE, span), jnp.float32)

        @pl.when(s >= 2)
        def _(c=c):
            onward[c][0].wait_recv()

        @pl.when(odd)
        def _(c=c, off=off):
            even_copies[c].wait_recv()

            def link(i, _):
                here = pl.ds(pl.multiple_of(i * tb, tb), tb)
                col = pl.ds(pl.multiple_of(off + i * tb, tb), tb)
                rates = rate[:, col]
                entering = carry[c, :, here]
                mine = jnp.exp2(rates * tot_in[c, :, here]) * entering + even_end[c, :, here]
                carry_out[c, :, here] = jnp.exp2(rates * tot[c, :, here]) * mine + ends[c, :, here]
                carry[c, :, here] = mine
                return 0

            lax.fori_loop(0, span // tb, link, 0)

        @pl.when(odd & (s < ns - 1))
        def _(c=c):
            onward[c][1].start()
            onward[c][0].start()

    def finish(c, r, off):
        def piece(i, _):
            here = pl.ds(pl.multiple_of(i * tb, tb), tb)
            col = pl.ds(pl.multiple_of(off + i * tb, tb), tb)
            gcol = pl.ds(pl.multiple_of(inner + off + i * tb, tb), tb)
            rates = rate[:, col]
            entering = carry[c, :, here]

            def eight(b, _):
                at = pl.ds(pl.multiple_of(b * 8, 8), 8)
                running = run[c, at, here]
                outs = []
                for k in range(8):
                    t = r * rows + b * 8 + k
                    outs.append(
                        jnp.sum(
                            jnp.exp2(rates * running[k : k + 1]) * (wide(csp[t], tb) * entering),
                            axis=0,
                            keepdims=True,
                        )
                    )
                acc[c, at, here] = acc[c, at, here] + jnp.concatenate(outs, axis=0)
                return 0

            lax.fori_loop(0, rows // 8, eight, 0)
            if r == 0:
                gate = clean[:, gcol].astype(jnp.float32)
            elif r == 1:
                gate = corrupt[:, gcol].astype(jnp.float32)
            else:
                gate = jnp.where(
                    take_gate, clean[:, gcol].astype(jnp.float32), corrupt[:, gcol].astype(jnp.float32)
                )
            silu = gate / (1.0 + jnp.exp(-gate))
            result = ((acc[c, :, here] + dsk[:, col] * act[r, :, col]) * silu).astype(jnp.bfloat16)
            if r < 2:
                cut[r, :, here] = result
            else:
                out[:, col] = result
            return 0

        lax.fori_loop(0, span // tb, piece, 0)

    finish(0, 0, v * span)
    finish(1, 1, v * span)
    for copy in cor_copies:
        copy.start()
    gap = cut[0].astype(jnp.float32) - cut[1].astype(jnp.float32)
    own_sq[...] = jnp.sum(gap * gap, axis=0, keepdims=True)
    start_all(own_sq, sq_in, s_sq, r_sq)
    for c in range(2, len(chunks)):
        finish(c, *chunks[c])
    for copy in cor_copies:
        copy.wait()

    def peak_at(theirs, place):
        col = pl.ds(pl.multiple_of(place * span, 128), span)
        own_pk[:, col] = jnp.max(
            jnp.abs(out[:, col].astype(jnp.float32) - theirs.astype(jnp.float32)), axis=0, keepdims=True
        )

    peak_at(cut[1], v)
    for d in range(1, nv):
        peak_at(whole[d - 1], lax.rem(v + nv - d, nv))
    start_all(own_pk, pk_in, s_pk, r_pk)
    wait_all(own_sq, sq_in, s_sq, r_sq)
    nrm[...] = own_sq[...] + jnp.sum(sq_in[...], axis=0)
    nrm_copies = [
        remote(nrm, nrm_in.at[d - 1], s_nrm.at[d - 1], r_nrm.at[d - 1], {"var": lax.rem(v + d, nv)})
        for d in range(1, nv)
    ]
    for copy in nrm_copies:
        copy.start()
    wait_all(own_pk, pk_in, s_pk, r_pk)
    best = jnp.maximum(own_pk[...], jnp.max(pk_in[...], axis=0))
    own_pk[...] = best
    for copy in nrm_copies:
        copy.wait()

    def settle(squares, place):
        col = pl.ds(pl.multiple_of(place * span, 128), span)
        eff[:, col] = own_pk[:, col] / jnp.sqrt(squares / (rows * ns) + TINY)

    settle(nrm[...], v)
    for d in range(1, nv):
        settle(nrm_in[d - 1], lax.rem(v + nv - d, nv))

    @pl.when(s < ns - 1)
    def _():
        rim_copy.wait_send()

    @pl.when(even)
    def _():
        tot_copy.wait_send()
        for copy in even_copies:
            copy.wait_send()

    @pl.when(odd & (s < ns - 1))
    def _():
        for pair in onward:
            pair[0].wait_send()
            pair[1].wait_send()


def shards(clean, corrupt, pos, mode, a_log, dtb, cw, cb, xw, dtw, dsk):
    ns, nv = lax.axis_size("seq"), lax.axis_size("var")
    rows = clean.shape[0]
    inner = cw.shape[1]
    span = inner // nv
    n = 2 + nv
    f32, b16 = jnp.float32, jnp.bfloat16
    vm = pltpu.VMEM
    dma = pltpu.SemaphoreType.DMA
    lb = lanes(inner, 256)
    out, eff = pl.pallas_call(
        functools.partial(body, ns, nv),
        out_shape=(
            jax.ShapeDtypeStruct((rows, inner), b16),
            jax.ShapeDtypeStruct((1, inner), f32),
        ),
        in_specs=[pl.BlockSpec(memory_space=vm)] * 11,
        out_specs=[pl.BlockSpec(memory_space=vm)] * 2,
        scratch_shapes=[
            vm((16, inner), b16), vm((16, inner), b16),
            vm((3, rows + PAD, lb), f32),
            vm((3 * rows, inner), b16), vm((3, rows, inner), f32),
            vm((3 * rows, 256), f32),
            vm((3 * rows, STATE, 128), f32), vm((3 * rows, STATE, 128), f32),
            vm((STATE, inner), f32),
            vm((n, rows, span), f32), vm((n, rows, span), f32), vm((n, rows, span), f32),
            vm((n, 1, span), f32), vm((n, 1, span), f32),
            vm((n, STATE, span), f32), vm((n, STATE, span), f32),
            vm((n, STATE, span), f32), vm((n, STATE, span), f32),
            vm((2, rows, span), b16), vm((nv - 1, rows, span), b16),
            vm((1, span), f32), vm((ns - 1, 1, span), f32),
            vm((1, inner), f32), vm((ns - 1, 1, inner), f32),
            vm((1, span), f32), vm((nv - 1, 1, span), f32),
            dma, dma, dma, dma,
            dma((n,)), dma((n,)), dma((n, 2)), dma((n,)),
            dma((nv - 1,)), dma((nv - 1,)),
            dma((ns - 1,)), dma((ns - 1,)), dma((ns - 1,)), dma((ns - 1,)),
            dma((nv - 1,)), dma((nv - 1,)),
        ],
        compiler_params=pltpu.CompilerParams(
            collective_id=0, has_side_effects=True, vmem_limit_bytes=60 * 1024 * 1024
        ),
    )(
        clean, corrupt, pos, mode.reshape(1, 1), a_log, dtb.reshape(1, -1), cw,
        cb.reshape(1, -1), xw, dtw, dsk.reshape(1, -1),
    )
    return (out[None], eff)


def solution(mesh):
    return jax.shard_map(
        shards,
        mesh=mesh,
        in_specs=(
            P("seq", None), P("seq", None), P("var", None), P("var"),
            P(), P(), P(), P(), P(), P(), P(),
        ),
        out_specs=(P("var", "seq", None), P("var", None)),
        check_vma=False,
    )
```

time: 366 us -> 84.5 us (0.23)
  blocking collectives: 211 us -> 0 us
  other arithmetic: 90.6 us -> 0 us
  Pallas kernels: 0 us -> 75.6 us
  local copies, waits for them, and re-layouts: 34.8 us -> 7.32 us
  between operations: 15.7 us -> 1.29 us
  starting transfers between devices: 4.95 us -> 0 us
  matrix products: 4.74 us -> 0 us
    all_gather x8 -> x0, blocking collectives: 211 us -> none  [the longest x4 138 us: prefix(): everything = jax.tree.map(lambda part: lax.all_gather(part, axis), value)]
    pallas_call x0 -> x1, Pallas kernels: none -> 75.6 us  [shards(): pl.pallas_call(functools.partial(body, ns, nv), out_shape=(jax.ShapeDtype...]
    select_n x17 -> x0, other arithmetic: 19.8 us -> none  [the longest x16 19.7 us: hop(): return jax.tree.map(lambda a, b: jnp.where(reached, a, b), new, before)]
    reduce_sum x37 -> x0, other arithmetic: 17 us -> none  [the longest x36 17 us: advance(): outputs.append(jnp.sum(c_rows[row][:, None] * state, axis=0))]
    slice x9 -> x0, other arithmetic: 16.1 us -> none  [the longest x8 13.8 us: advance(): flows[row][None, :] * b_rows[row][:, None]]
    neg x6 -> x0, other arithmetic: 12.3 us -> none  [the longest x4 10.5 us: advance(): -steps[row][None, :] * decay_rates]
    convert_element_type x7 -> x0, other arithmetic: 10.9 us -> none  [the longest x3 7.37 us: finish(): ((readout + skip_cut[None, :] * signal_f) * gate_act).astype(jnp.bfloat16)]
    dynamic_slice x30 -> x0, local copies, waits for them, and re-layouts: 10.8 us -> none  [the longest x12 8.26 us: local_pass(): lax.scan(advance, jnp.zeros((STATE, span), jnp.float32), pieces)]
  transfers between devices with their start and end apart: 3 -> 0, of which waited for: 0 -> 0; matrix products, arithmetic and copies ran while one was open for 20% -> 0% of each run, Pallas kernels for 0% -> 0%
where the time goes in v1:
time: 84.5 us; the launch traced here: 84.2 us
  Pallas kernels  75.6 us (89%)
  local copies, waits for them, and re-layouts  7.32 us (9%)
  between operations  1.29 us (2%)
    pallas_call x1, Pallas kernels, shards(): pl.pallas_call(functools.partial(body, ns, nv), out_shape=(jax.ShapeDtype...  75.6 us
    unnamed x3, local copies, waits for them, and re-layouts  7.32 us

profile of v1, /device:TPU:0, one launch (start us, length us, event | category | flops | bytes accessed | tf_op | source)
XLA Modules:
  0.0 84.2 jit_solution(6242290079963672853)
XLA Ops:
  1.3 4.3 %copy.13.xw = bf16[5120,192]{1,0:T(8,128)(2,1)} copy(bf16[5120,192]{0,1:T(8,128)(2,1)} %param.19) | data formatting | bytes 3932160 | tf_op args[8]
  5.5 75.6 %shard_map.122 = (bf16[32,5120]{1,0:T(8,128)(2,1)}, f32[1,5120]{1,0:T(1,128)}) custom-call(bf16[32,10240]{1,0:T(8,128)(2,1)} %clean.1, bf16[32,10240]{1,0:T(8,128)(2,1)} %corrupt.1, s32[1,16]{1,0:T(1,128)} %pos.1, s32[1,1]{1,0:T(1,128)} %bitcast.5.mode, f32[16,5120]{1,0:T(8,128)} %a_log.1, f32[1,5120]{1,0:T(1,128)} %bitcast.7, f32[4,5120]{1,0:T(4,128)} %cw.1, ...), custom_call_target="tpu_custom_call" | custom-call | tf_op jit(solution)/shard_map/pallas_call | solution.py:365
  81.2 1.7 %copy.17 = bf16[1,32,5120]{2,1,0:T(8,128)(2,1)} copy(bf16[1,32,5120]{2,1,0:T(8,128)(2,1)} %bitcast.6) | data formatting | bytes 655360
  82.9 1.3 %copy.18 = f32[1,5120]{1,0:T(1,128)} copy(f32[1,5120]{1,0:T(1,128)} %get-tuple-element.9) | data formatting | bytes 40960

commit v2 on v1

--- a/solution.py
+++ b/solution.py
@@ -32,8 +32,8 @@
     clean, corrupt, pos, mode, a_log, dtb, cw, cb, xw, dtw, dsk,
     out, eff,
     tails, rims, ext, act16, act, proj, bsp, csp, rate, stp, acc, run, tot, tot_in,
-    ends, even_end, carry, carry_out, cut, whole, own_sq, sq_in, own_pk, pk_in, nrm, nrm_in,
-    s_rim, r_rim, s_tot, r_tot, s_even, r_even, s_car, r_car, s_cor, r_cor,
+    ends, even_end, carry, carry_out, inflow, cut, whole, own_sq, sq_in, own_pk, pk_in, nrm, nrm_all,
+    s_rim, r_rim, s_tot, r_tot, s_even, r_even, s_car, s_back, r_car, s_cor, r_cor,
     s_sq, r_sq, s_pk, r_pk, s_nrm, r_nrm,
 ):
     rows = clean.shape[0]
@@ -55,12 +55,11 @@
     for d in range(1, nv):
         pl.semaphore_signal(barrier, inc=1, device_id={"var": lax.rem(v + d, nv)}, device_id_type=MESH)
 
-    tails[...] = jnp.concatenate(
-        [
-            clean[rows - 16 :, :inner].astype(jnp.float32)[8:],
-            corrupt[rows - 16 :, :inner].astype(jnp.float32)[8:],
-        ],
-        axis=0,
+    row_of = lax.broadcasted_iota(jnp.int32, (8, inner), 0)
+    tails[...] = jnp.where(
+        row_of > 4,
+        clean[rows - 16 :, :inner].astype(jnp.float32)[8:],
+        pltpu.roll(corrupt[rows - 16 :, :inner].astype(jnp.float32)[8:], 4, 0),
     ).astype(jnp.bfloat16)
     pl.semaphore_wait(barrier, ns - 1 + nv - 1)
 
@@ -96,8 +95,8 @@
     def conv(i, _):
         col = pl.ds(pl.multiple_of(i * lb, lb), lb)
         edge = rims[:, col].astype(jnp.float32)
-        ext[0, 0:PAD, :] = edge[0:8]
-        ext[1, 0:PAD, :] = edge[8:16]
+        ext[0, 0:PAD, :] = edge
+        ext[1, 0:PAD, :] = pltpu.roll(edge, 4, 0)
         ext[0, PAD:, :] = clean[:, col].astype(jnp.float32)
         ext[1, PAD:, :] = corrupt[:, col].astype(jnp.float32)
         ext[2] = jnp.where(take_signal, ext[0], ext[1])
@@ -112,9 +111,11 @@
         return 0
 
     lax.fori_loop(0, inner // lb, conv, 0)
-    width = xw.shape[1]
+    width = xw.shape[0]
     proj[...] = jnp.zeros_like(proj)
-    proj[:, :width] = jnp.dot(act16[...], xw[...], preferred_element_type=jnp.float32)
+    proj[:, :width] = lax.dot_general(
+        act16[...], xw[...], (((1,), (1,)), ((), ())), preferred_element_type=jnp.float32
+    )
     flipped = proj[:, 128:].T
     first = RANK - 128
     for t in range(3 * rows):
@@ -123,6 +124,10 @@
 
     chunks = [(0, v * span), (1, v * span)] + [(2, j * span) for j in range(nv)]
     tb = lanes(span, 256)
+
+    partner = {"seq": lax.rem(s + 1, ns)}
+    tot_copies = [remote(tot.at[c], tot_in.at[c], s_tot.at[c], r_tot.at[c], partner) for c in range(len(chunks))]
+    even_copies = [remote(ends.at[c], even_end.at[c], s_even.at[c], r_even.at[c], partner) for c in range(len(chunks))]
 
     for c, (r, off) in enumerate(chunks):
         low = proj[r * rows : (r + 1) * rows, :RANK].astype(jnp.bfloat16)
@@ -138,16 +143,9 @@
 
         lax.fori_loop(0, span // tb, steps_of, 0)
 
-    partner = {"seq": lax.rem(s + 1, ns)}
-    tot_copy = remote(tot, tot_in, s_tot, r_tot, partner)
-
-    @pl.when(even)
-    def _():
-        tot_copy.start()
-
-    even_copies = [remote(ends.at[c], even_end.at[c], s_even.at[c], r_even.at[c], partner) for c in range(len(chunks))]
-
-    for c, (r, off) in enumerate(chunks):
+        @pl.when(even)
+        def _(c=c):
+            tot_copies[c].start()
 
         def scan_of(i, _, c=c, r=r, off=off):
             here = pl.ds(pl.multiple_of(i * tb, tb), tb)
@@ -182,71 +180,71 @@
         def _(c=c):
             even_copies[c].start()
 
-    @pl.when(odd)
-    def _():
-        tot_copy.wait_recv()
-
-    onward = []
-    for c in range(len(chunks)):
-        onward.append(
-            [
-                remote(carry_out.at[c], carry.at[c], s_car.at[c, m], r_car.at[c], {"seq": lax.rem(s + 1 + m, ns)})
-                for m in range(2)
-            ]
-        )
+    onward = [
+        remote(carry_out.at[c], carry.at[c], s_car.at[c], r_car.at[c], {"seq": lax.rem(s + 2, ns)})
+        for c in range(len(chunks))
+    ]
+    beside = [
+        remote(carry.at[c], carry.at[c], s_back.at[c], r_car.at[c], {"seq": lax.rem(s + ns - 1, ns)})
+        for c in range(len(chunks))
+    ]
 
     cor_copies = [
-        remote(cut.at[1], whole.at[d - 1], s_cor.at[d - 1], r_cor.at[d - 1], {"var": lax.rem(v + d, nv)})
+        remote(cut.at[1], whole.at[v], s_cor.at[d - 1], r_cor.at[d - 1], {"var": lax.rem(v + d, nv)})
         for d in range(1, nv)
     ]
 
-    def seq_copy(d, src, dst, send, recv):
-        return remote(src, dst.at[d - 1], send.at[d - 1], recv.at[d - 1], {"seq": lax.rem(s + d, ns)})
-
-    def start_all(src, dst, send, recv):
+    def sq_copy(d):
+        return remote(own_sq, sq_in.at[d - 1], s_sq.at[d - 1], r_sq.at[d - 1], {"seq": lax.rem(s + d, ns)})
+
+    def pk_copy(d, j):
+        return remote(
+            own_pk.at[j], pk_in.at[d - 1, j], s_pk.at[d - 1, j], r_pk.at[d - 1, j], {"seq": lax.rem(s + d, ns)}
+        )
+
+    def each(act_on):
         def go(d, _):
-            seq_copy(d, src, dst, send, recv).start()
+            act_on(d)
             return 0
 
         lax.fori_loop(1, ns, go, 0)
 
-    def wait_all(src, dst, send, recv):
-        def go(d, _):
-            seq_copy(d, src, dst, send, recv).wait()
-            return 0
-
-        lax.fori_loop(1, ns, go, 0)
-
-    for c, (r, off) in enumerate(chunks):
-
+    def enter(c, r, off):
         @pl.when(s < 2)
-        def _(c=c):
+        def _():
             carry[c] = jnp.zeros((STATE, span), jnp.float32)
 
         @pl.when(s >= 2)
-        def _(c=c):
-            onward[c][0].wait_recv()
+        def _():
+            onward[c].wait_recv()
 
         @pl.when(odd)
-        def _(c=c, off=off):
+        def _():
+            @pl.when(s >= 2)
+            def _():
+                beside[c].start()
+
+            tot_copies[c].wait_recv()
             even_copies[c].wait_recv()
 
             def link(i, _):
                 here = pl.ds(pl.multiple_of(i * tb, tb), tb)
                 col = pl.ds(pl.multiple_of(off + i * tb, tb), tb)
                 rates = rate[:, col]
-                entering = carry[c, :, here]
-                mine = jnp.exp2(rates * tot_in[c, :, here]) * entering + even_end[c, :, here]
+                mine = jnp.exp2(rates * tot_in[c, :, here]) * carry[c, :, here] + even_end[c, :, here]
                 carry_out[c, :, here] = jnp.exp2(rates * tot[c, :, here]) * mine + ends[c, :, here]
-                carry[c, :, here] = mine
+                inflow[c, :, here] = mine
                 return 0
 
             lax.fori_loop(0, span // tb, link, 0)
 
-        @pl.when(odd & (s < ns - 1))
-        def _(c=c):
-            onward[c][1].start()
-            onward[c][0].start()
+            @pl.when(s < ns - 1)
+            def _():
+                onward[c].start()
+
+        @pl.when(even)
+        def _():
+            inflow[c] = carry[c]
 
     def finish(c, r, off):
         def piece(i, _):
@@ -254,7 +252,7 @@
             col = pl.ds(pl.multiple_of(off + i * tb, tb), tb)
             gcol = pl.ds(pl.multiple_of(inner + off + i * tb, tb), tb)
             rates = rate[:, col]
-            entering = carry[c, :, here]
+            entering = inflow[c, :, here]
 
             def eight(b, _):
                 at = pl.ds(pl.multiple_of(b * 8, 8), 8)
@@ -291,49 +289,41 @@
 
         lax.fori_loop(0, span // tb, piece, 0)
 
-    finish(0, 0, v * span)
-    finish(1, 1, v * span)
+    for c in range(2):
+        enter(c, *chunks[c])
+        finish(c, *chunks[c])
     for copy in cor_copies:
         copy.start()
+    whole[v] = cut[1]
     gap = cut[0].astype(jnp.float32) - cut[1].astype(jnp.float32)
     own_sq[...] = jnp.sum(gap * gap, axis=0, keepdims=True)
-    start_all(own_sq, sq_in, s_sq, r_sq)
-    for c in range(2, len(chunks)):
-        finish(c, *chunks[c])
-    for copy in cor_copies:
-        copy.wait()
-
-    def peak_at(theirs, place):
-        col = pl.ds(pl.multiple_of(place * span, 128), span)
-        own_pk[:, col] = jnp.max(
-            jnp.abs(out[:, col].astype(jnp.float32) - theirs.astype(jnp.float32)), axis=0, keepdims=True
-        )
-
-    peak_at(cut[1], v)
-    for d in range(1, nv):
-        peak_at(whole[d - 1], lax.rem(v + nv - d, nv))
-    start_all(own_pk, pk_in, s_pk, r_pk)
-    wait_all(own_sq, sq_in, s_sq, r_sq)
-    nrm[...] = own_sq[...] + jnp.sum(sq_in[...], axis=0)
+    each(lambda d: sq_copy(d).start())
     nrm_copies = [
-        remote(nrm, nrm_in.at[d - 1], s_nrm.at[d - 1], r_nrm.at[d - 1], {"var": lax.rem(v + d, nv)})
+        remote(nrm, nrm_all.at[v], s_nrm.at[d - 1], r_nrm.at[d - 1], {"var": lax.rem(v + d, nv)})
         for d in range(1, nv)
     ]
-    for copy in nrm_copies:
-        copy.start()
-    wait_all(own_pk, pk_in, s_pk, r_pk)
-    best = jnp.maximum(own_pk[...], jnp.max(pk_in[...], axis=0))
-    own_pk[...] = best
+    for j in range(nv):
+        c = 2 + j
+        enter(c, *chunks[c])
+        finish(c, *chunks[c])
+        if j == 0:
+            for copy in cor_copies:
+                copy.wait()
+        if j == nv - 1:
+            each(lambda d: sq_copy(d).wait())
+            nrm[...] = own_sq[...] + jnp.sum(sq_in[...], axis=0)
+            for copy in nrm_copies:
+                copy.start()
+            nrm_all[v] = nrm[...]
+        mine = out[:, j * span : (j + 1) * span].astype(jnp.float32)
+        own_pk[j] = jnp.max(jnp.abs(mine - whole[j].astype(jnp.float32)), axis=0, keepdims=True)
+        each(lambda d, j=j: pk_copy(d, j).start())
     for copy in nrm_copies:
         copy.wait()
-
-    def settle(squares, place):
-        col = pl.ds(pl.multiple_of(place * span, 128), span)
-        eff[:, col] = own_pk[:, col] / jnp.sqrt(squares / (rows * ns) + TINY)
-
-    settle(nrm[...], v)
-    for d in range(1, nv):
-        settle(nrm_in[d - 1], lax.rem(v + nv - d, nv))
+    for j in range(nv):
+        each(lambda d, j=j: pk_copy(d, j).wait())
+        best = jnp.maximum(own_pk[j], jnp.max(pk_in[:, j], axis=0))
+        eff[:, j * span : (j + 1) * span] = best / jnp.sqrt(nrm_all[j] / (rows * ns) + TINY)
 
     @pl.when(s < ns - 1)
     def _():
@@ -341,15 +331,19 @@
 
     @pl.when(even)
     def _():
-        tot_copy.wait_send()
-        for copy in even_copies:
+        for c in range(len(chunks)):
+            tot_copies[c].wait_send()
+            even_copies[c].wait_send()
+
+    @pl.when(odd & (s >= 2))
+    def _():
+        for copy in beside:
             copy.wait_send()
 
     @pl.when(odd & (s < ns - 1))
     def _():
-        for pair in onward:
-            pair[0].wait_send()
-            pair[1].wait_send()
+        for copy in onward:
+            copy.wait_send()
 
 
 def shards(clean, corrupt, pos, mode, a_log, dtb, cw, cb, xw, dtw, dsk):
@@ -371,7 +365,7 @@
         in_specs=[pl.BlockSpec(memory_space=vm)] * 11,
         out_specs=[pl.BlockSpec(memory_space=vm)] * 2,
         scratch_shapes=[
-            vm((16, inner), b16), vm((16, inner), b16),
+            vm((8, inner), b16), vm((8, inner), b16),
             vm((3, rows + PAD, lb), f32),
             vm((3 * rows, inner), b16), vm((3, rows, inner), f32),
             vm((3 * rows, 256), f32),
@@ -380,15 +374,15 @@
             vm((n, rows, span), f32), vm((n, rows, span), f32), vm((n, rows, span), f32),
             vm((n, 1, span), f32), vm((n, 1, span), f32),
             vm((n, STATE, span), f32), vm((n, STATE, span), f32),
-            vm((n, STATE, span), f32), vm((n, STATE, span), f32),
-            vm((2, rows, span), b16), vm((nv - 1, rows, span), b16),
+            vm((n, STATE, span), f32), vm((n, STATE, span), f32), vm((n, STATE, span), f32),
+            vm((2, rows, span), b16), vm((nv, rows, span), b16),
             vm((1, span), f32), vm((ns - 1, 1, span), f32),
-            vm((1, inner), f32), vm((ns - 1, 1, inner), f32),
-            vm((1, span), f32), vm((nv - 1, 1, span), f32),
-            dma, dma, dma, dma,
-            dma((n,)), dma((n,)), dma((n, 2)), dma((n,)),
+            vm((nv, 1, span), f32), vm((ns - 1, nv, 1, span), f32),
+            vm((1, span), f32), vm((nv, 1, span), f32),
+            dma, dma, dma((n,)), dma((n,)),
+            dma((n,)), dma((n,)), dma((n,)), dma((n,)), dma((n,)),
             dma((nv - 1,)), dma((nv - 1,)),
-            dma((ns - 1,)), dma((ns - 1,)), dma((ns - 1,)), dma((ns - 1,)),
+            dma((ns - 1,)), dma((ns - 1,)), dma((ns - 1, nv)), dma((ns - 1, nv)),
             dma((nv - 1,)), dma((nv - 1,)),
         ],
         compiler_params=pltpu.CompilerParams(
@@ -396,7 +390,7 @@
         ),
     )(
         clean, corrupt, pos, mode.reshape(1, 1), a_log, dtb.reshape(1, -1), cw,
-        cb.reshape(1, -1), xw, dtw, dsk.reshape(1, -1),
+        cb.reshape(1, -1), xw.T, dtw, dsk.reshape(1, -1),
     )
     return (out[None], eff)
 

time: 84.5 us -> 68.5 us (0.81)
  Pallas kernels: 75.6 us -> 63.9 us
  local copies, waits for them, and re-layouts: 7.32 us -> 3.05 us
    pallas_call x1, Pallas kernels: 75.6 us -> 63.9 us  [shards(): pl.pallas_call(functools.partial(body, ns, nv), out_shape=(jax.ShapeDtype...]
    unnamed x3 -> x2, local copies, waits for them, and re-layouts: 7.32 us -> 3.05 us
where the time goes in v2:
time: 68.5 us; the launch traced here: 68.3 us
  Pallas kernels  63.9 us (93%)
  local copies, waits for them, and re-layouts  3.05 us (4%)
  between operations  1.29 us (2%)
    pallas_call x1, Pallas kernels, shards(): pl.pallas_call(functools.partial(body, ns, nv), out_shape=(jax.ShapeDtype...  63.9 us
    unnamed x2, local copies, waits for them, and re-layouts  3.05 us

profile of v2, /device:TPU:0, one launch (start us, length us, event | category | flops | bytes accessed | tf_op | source)
XLA Modules:
  0.0 68.3 jit_solution(1698173121440244940)
XLA Ops:
  1.3 63.9 %shard_map.122 = (bf16[32,5120]{1,0:T(8,128)(2,1)}, f32[1,5120]{1,0:T(1,128)}) custom-call(bf16[32,10240]{1,0:T(8,128)(2,1)} %clean.1, bf16[32,10240]{1,0:T(8,128)(2,1)} %corrupt.1, s32[1,16]{1,0:T(1,128)} %pos.1, s32[1,1]{1,0:T(1,128)} %bitcast.6.mode, f32[16,5120]{1,0:T(8,128)} %a_log.1, f32[1,5120]{1,0:T(1,128)} %bitcast.9, f32[4,5120]{1,0:T(4,128)} %cw.1, ...), custom_call_target="tpu_custom_call" | custom-call | tf_op jit(solution)/shard_map/pallas_call | solution.py:359
  65.2 1.7 %copy.16 = bf16[1,32,5120]{2,1,0:T(8,128)(2,1)} copy(bf16[1,32,5120]{2,1,0:T(8,128)(2,1)} %bitcast.8) | data formatting | bytes 655360
  66.9 1.3 %copy.17 = f32[1,5120]{1,0:T(1,128)} copy(f32[1,5120]{1,0:T(1,128)} %get-tuple-element.9) | data formatting | bytes 40960

commit v3 on v2

--- a/solution.py
+++ b/solution.py
@@ -129,6 +129,61 @@
     tot_copies = [remote(tot.at[c], tot_in.at[c], s_tot.at[c], r_tot.at[c], partner) for c in range(len(chunks))]
     even_copies = [remote(ends.at[c], even_end.at[c], s_even.at[c], r_even.at[c], partner) for c in range(len(chunks))]
 
+    onward = [
+        remote(carry_out.at[c], carry.at[c], s_car.at[c], r_car.at[c], {"seq": lax.rem(s + 2, ns)})
+        for c in range(len(chunks))
+    ]
+    beside = [
+        remote(carry.at[c], carry.at[c], s_back.at[c], r_car.at[c], {"seq": lax.rem(s + ns - 1, ns)})
+        for c in range(len(chunks))
+    ]
+
+    def enter(c, r, off):
+        @pl.when(s < 2)
+        def _():
+            carry[c] = jnp.zeros((STATE, span), jnp.float32)
+
+        @pl.when(s >= 2)
+        def _():
+            onward[c].wait_recv()
+
+        @pl.when(odd)
+        def _():
+            @pl.when(s >= 2)
+            def _():
+                beside[c].start()
+
+            tot_copies[c].wait_recv()
+            even_copies[c].wait_recv()
+
+            def link(i, _):
+                here = pl.ds(pl.multiple_of(i * tb, tb), tb)
+                col = pl.ds(pl.multiple_of(off + i * tb, tb), tb)
+                rates = rate[:, col]
+                mine = jnp.exp2(rates * tot_in[c, :, here]) * carry[c, :, here] + even_end[c, :, here]
+                carry_out[c, :, here] = jnp.exp2(rates * tot[c, :, here]) * mine + ends[c, :, here]
+                inflow[c, :, here] = mine
+                return 0
+
+            lax.fori_loop(0, span // tb, link, 0)
+
+            @pl.when(s < ns - 1)
+            def _():
+                onward[c].start()
+
+        @pl.when(even)
+        def _():
+            inflow[c] = carry[c]
+
+    early = ((0, 2, 2), (2, 4, 4))
+
+    def enter_late(c):
+        begin = max([0] + [high for _, high, lag in early if c < len(chunks) - lag])
+
+        @pl.when(s >= begin)
+        def _():
+            enter(c, *chunks[c])
+
     for c, (r, off) in enumerate(chunks):
         low = proj[r * rows : (r + 1) * rows, :RANK].astype(jnp.bfloat16)
 
@@ -180,14 +235,12 @@
         def _(c=c):
             even_copies[c].start()
 
-    onward = [
-        remote(carry_out.at[c], carry.at[c], s_car.at[c], r_car.at[c], {"seq": lax.rem(s + 2, ns)})
-        for c in range(len(chunks))
-    ]
-    beside = [
-        remote(carry.at[c], carry.at[c], s_back.at[c], r_car.at[c], {"seq": lax.rem(s + ns - 1, ns)})
-        for c in range(len(chunks))
-    ]
+        for low_s, high_s, lag in early:
+            if c >= lag:
+
+                @pl.when((s >= low_s) & (s < high_s))
+                def _(c=c - lag):
+                    enter(c, *chunks[c])
 
     cor_copies = [
         remote(cut.at[1], whole.at[v], s_cor.at[d - 1], r_cor.at[d - 1], {"var": lax.rem(v + d, nv)})
@@ -208,43 +261,6 @@
             return 0
 
         lax.fori_loop(1, ns, go, 0)
-
-    def enter(c, r, off):
-        @pl.when(s < 2)
-        def _():
-            carry[c] = jnp.zeros((STATE, span), jnp.float32)
-
-        @pl.when(s >= 2)
-        def _():
-            onward[c].wait_recv()
-
-        @pl.when(odd)
-        def _():
-            @pl.when(s >= 2)
-            def _():
-                beside[c].start()
-
-            tot_copies[c].wait_recv()
-            even_copies[c].wait_recv()
-
-            def link(i, _):
-                here = pl.ds(pl.multiple_of(i * tb, tb), tb)
-                col = pl.ds(pl.multiple_of(off + i * tb, tb), tb)
-                rates = rate[:, col]
-                mine = jnp.exp2(rates * tot_in[c, :, here]) * carry[c, :, here] + even_end[c, :, here]
-                carry_out[c, :, here] = jnp.exp2(rates * tot[c, :, here]) * mine + ends[c, :, here]
-                inflow[c, :, here] = mine
-                return 0
-
-            lax.fori_loop(0, span // tb, link, 0)
-
-            @pl.when(s < ns - 1)
-            def _():
-                onward[c].start()
-
-        @pl.when(even)
-        def _():
-            inflow[c] = carry[c]
 
     def finish(c, r, off):
         def piece(i, _):
@@ -290,7 +306,7 @@
         lax.fori_loop(0, span // tb, piece, 0)
 
     for c in range(2):
-        enter(c, *chunks[c])
+        enter_late(c)
         finish(c, *chunks[c])
     for copy in cor_copies:
         copy.start()
@@ -304,7 +320,7 @@
     ]
     for j in range(nv):
         c = 2 + j
-        enter(c, *chunks[c])
+        enter_late(c)
         finish(c, *chunks[c])
         if j == 0:
             for copy in cor_copies:

time: 68.5 us -> 67.5 us (0.985)
  Pallas kernels: 63.9 us -> 62.9 us
    pallas_call x1, Pallas kernels: 63.9 us -> 62.9 us  [shards(): pl.pallas_call(functools.partial(body, ns, nv), out_shape=(jax.ShapeDtype...]
where the time goes in v3:
time: 67.5 us; the launch traced here: 67.2 us
  Pallas kernels  62.9 us (93%)
  local copies, waits for them, and re-layouts  3.05 us (5%)
  between operations  1.29 us (2%)
    pallas_call x1, Pallas kernels, shards(): pl.pallas_call(functools.partial(body, ns, nv), out_shape=(jax.ShapeDtype...  62.9 us
    unnamed x2, local copies, waits for them, and re-layouts  3.05 us

profile of v3, /device:TPU:0, one launch (start us, length us, event | category | flops | bytes accessed | tf_op | source)
XLA Modules:
  0.0 67.2 jit_solution(9992971583788972845)
XLA Ops:
  1.3 62.9 %shard_map.122 = (bf16[32,5120]{1,0:T(8,128)(2,1)}, f32[1,5120]{1,0:T(1,128)}) custom-call(bf16[32,10240]{1,0:T(8,128)(2,1)} %clean.1, bf16[32,10240]{1,0:T(8,128)(2,1)} %corrupt.1, s32[1,16]{1,0:T(1,128)} %pos.1, s32[1,1]{1,0:T(1,128)} %bitcast.6.mode, f32[16,5120]{1,0:T(8,128)} %a_log.1, f32[1,5120]{1,0:T(1,128)} %bitcast.9, f32[4,5120]{1,0:T(4,128)} %cw.1, ...), custom_call_target="tpu_custom_call" | custom-call | tf_op jit(solution)/shard_map/pallas_call | solution.py:375
  64.2 1.7 %copy.16 = bf16[1,32,5120]{2,1,0:T(8,128)(2,1)} copy(bf16[1,32,5120]{2,1,0:T(8,128)(2,1)} %bitcast.8) | data formatting | bytes 655360
  65.9 1.3 %copy.17 = f32[1,5120]{1,0:T(1,128)} copy(f32[1,5120]{1,0:T(1,128)} %get-tuple-element.9) | data formatting | bytes 40960
